TPU v7x, 256 devices: a whole 4x4x8 slice. The times are simulated.
256 devices in a mesh: band: 16 (over z, y_lo), col: 16 (over x, y_hi, core).
Axes of the slice: x: 4, y: 4 (y_hi: 2, y_lo: 2; y = y_hi * 2 + y_lo), z: 8, core: 2. Of those that a mesh axis runs over, the one named last changes fastest.
Arguments:
- valence_wave: bfloat16 [16, 96, 9216], P('band', 'col'), may hold values from -6 to 6
- conduction_wave: bfloat16 [16, 96, 9216], P('band', 'col'), may hold values from -6 to 6
- valence_index: int32 [16], replicated, may hold values from 0 to 4095
- occupied_energy: float32 [4096], replicated, may hold values from -6 to -0.5
- conduction_energy: float32 [16], replicated, may hold values from 0.5 to 8
- frequency: float32 [4], replicated, may hold values from 0.5 to 16
- gvec_cell: int32 [32768], P('col'), may hold values from 0 to 55295, as said below
- block_cell: int32 [16], P('col'), may hold values from 0 to 55295, as said below
Outputs:
- chi: float32 [32768, 128], P(('col', 'band'))
Inputs may be any that keep to these rules, and one draw needn't show every extreme that they name: `gvec_cell`: for rows j of owner k (k * 2048 <= j < (k + 1) * 2048) the entry is (kx 6 + ky - k * 6) * 96 + kz for the G vector's grid point (kx, ky, kz), whose ky lies in [k * 6, (k + 1) * 6); no point appears twice among the rows and block columns of one owner. `block_cell`: block column m has owner k = m // 1 and is encoded as for gvec_cell; its points differ from every row point of the same owner.
All inputs are finite; a program needn't handle non-finite values.
Results may differ from a plain program's by a relative error of at most 0.018.
Values may be sent and summed in bfloat16 or wider, within the bound.
No kernel may reach another device: no remote copies, remote signals or barrier semaphores. Data moves between devices by JAX's collectives and lax.ppermute only.
A program may use at most 128 MiB of HBM per device.

v0:
```python
import math
import jax
import jax.numpy as jnp
from jax import lax
from jax.sharding import PartitionSpec as P

GY = 96


def joined_along(pieces, dim):
    dims = list(pieces.shape[1:])
    dims[dim] *= pieces.shape[0]
    return jnp.moveaxis(pieces, 0, dim).reshape(dims)


def copy_for_each(x, axis):
    devices = lax.axis_size(axis)
    return lax.all_to_all(jnp.broadcast_to(x[None], (devices, *x.shape)), axis, 0, 0, tiled=True)


def collect(x, axis, dim):
    return joined_along(copy_for_each(x, axis), dim)


def cut_along(x, dim, devices):
    dims = x.shape
    pieces = x.reshape(*dims[:dim], devices, dims[dim] // devices, *dims[dim + 1 :])
    return jnp.moveaxis(pieces, dim, 0)


def sent_and_summed(x, axis, dim):
    pieces = cut_along(x, dim, lax.axis_size(axis))
    arrived = lax.all_to_all(pieces, axis, split_axis=0, concat_axis=0, tiled=True)
    return arrived.astype(jnp.float32).sum(axis=0)


def dft_tables(length, factor, out_type):
    indices = jnp.arange(length, dtype=jnp.int32)
    phases = indices[:, None] * indices[None, :] % length
    angles = phases.astype(jnp.float32) * (2.0 * math.pi / length)
    return (
        (jnp.cos(angles) * factor).astype(out_type),
        (-jnp.sin(angles) * factor).astype(out_type),
    )


def weighted_columns(block, weights):
    columns = block.astype(jnp.float32)
    stacked = jnp.stack([columns, jnp.stack([-columns[1], columns[0]])])
    scaled = stacked[None] * weights[:, None, None, :, None]
    scaled = scaled.transpose(2, 3, 0, 1, 4).astype(jnp.bfloat16)
    return scaled.reshape(2, block.shape[1], -1)


def pair_weights(
    pair_ids, valence_energy, conduction_energy, frequency, per_band, pairs_dev, norm_factor
):
    band_of = pair_ids // pairs_dev
    within = pair_ids % pairs_dev
    valence_of = within // per_band
    conduction_of = band_of * per_band + within % per_band
    valence_range = jnp.arange(valence_energy.shape[0], dtype=jnp.int32)
    conduction_range = jnp.arange(conduction_energy.shape[0], dtype=jnp.int32)
    valence_pick = jnp.sum(
        jnp.where(valence_of[:, None] == valence_range[None, :], valence_energy[None, :], 0.0),
        axis=1,
    )
    conduction_pick = jnp.sum(
        jnp.where(
            conduction_of[:, None] == conduction_range[None, :], conduction_energy[None, :], 0.0
        ),
        axis=1,
    )
    gap = conduction_pick - valence_pick
    freq_column = frequency[:, None]
    return (
        -4.0
        * gap[None, :]
        / (gap[None, :] * gap[None, :] + freq_column * freq_column)
        * norm_factor
    )


def per_device(
    valence_wave,
    conduction_wave,
    valence_index,
    occupied_energy,
    conduction_energy,
    frequency,
    gvec_cell,
    block_cell,
):
    local_valence, slab_x, plane_size = valence_wave.shape
    per_band = conduction_wave.shape[0]
    band_count = lax.axis_size("band")
    col_count = lax.axis_size("col")
    grid_x = slab_x * col_count
    grid_y = GY
    grid_z = plane_size // grid_y
    total_valence = local_valence * band_count
    pairs_dev = total_valence * per_band
    total_conduction = conduction_energy.shape[0]
    norm_factor = 1.0 / math.sqrt(total_valence * total_conduction)
    high = lax.Precision.HIGH
    z_cosine, z_sine = dft_tables(grid_z, 1.0, jnp.float32)
    y_cosine, y_sine = dft_tables(grid_y, 1.0 / math.sqrt(grid_y * grid_z), jnp.float32)
    x_cosine, x_sine = dft_tables(grid_x, 1.0 / math.sqrt(grid_x), jnp.bfloat16)
    x_table = jnp.stack([jnp.stack([x_cosine, -x_sine]), jnp.stack([x_sine, x_cosine])])
    conduction_float = conduction_wave.astype(jnp.float32)
    products = (
        collect(valence_wave, "band", 0).astype(jnp.float32)[:, None] * conduction_float[None]
    )
    products = products.reshape(-1, slab_x, grid_y, grid_z)
    z_real = jnp.einsum("kz,pxyz->pxyk", z_cosine, products, precision=high)
    z_imag = jnp.einsum("kz,pxyz->pxyk", z_sine, products, precision=high)
    y_real = jnp.einsum("jy,pxyk->pxjk", y_cosine, z_real, precision=high) - jnp.einsum(
        "jy,pxyk->pxjk", y_sine, z_imag, precision=high
    )
    y_imag = jnp.einsum("jy,pxyk->pxjk", y_sine, z_real, precision=high) + jnp.einsum(
        "jy,pxyk->pxjk", y_cosine, z_imag, precision=high
    )
    planes = jnp.stack([y_real, y_imag]).astype(jnp.bfloat16)
    exchanged = lax.all_to_all(planes, "col", split_axis=3, concat_axis=2, tiled=True)
    items = exchanged.shape[1]
    flat = exchanged.reshape(2, items, grid_x, -1)
    density = jnp.einsum(
        "orkx,rpxf->opkf", x_table, flat, preferred_element_type=jnp.float32
    ).astype(jnp.bfloat16)
    density = density.reshape(2, items, -1)
    row_density = jnp.take(density, gvec_cell, axis=2)
    block_density = jnp.take(density, block_cell, axis=2)
    block_all = collect(block_density, "col", 2)
    occupied_range = jnp.arange(occupied_energy.shape[0], dtype=jnp.int32)
    valence_energy = jnp.sum(
        jnp.where(valence_index[:, None] == occupied_range[None, :], occupied_energy[None, :], 0.0),
        axis=1,
    )
    pair_ids = lax.axis_index("band") * pairs_dev + jnp.arange(pairs_dev, dtype=jnp.int32)
    weights = pair_weights(
        pair_ids, valence_energy, conduction_energy, frequency, per_band, pairs_dev, norm_factor
    )
    right_side = weighted_columns(block_all, weights)
    return sent_and_summed(
        jnp.einsum(
            "rpg,rpc->gc", row_density, right_side, preferred_element_type=jnp.float32
        ).astype(jnp.bfloat16),
        "band",
        0,
    )


def solution(mesh):
    return jax.shard_map(
        per_device,
        mesh=mesh,
        in_specs=(
            P("band", "col", None),
            P("band", "col", None),
            P(),
            P(),
            P(),
            P(),
            P("col"),
            P("col"),
        ),
        out_specs=P(("col", "band"), None),
        check_vma=False,
    )
```

profile of v0, /device:TPU:2, one launch (start us, length us, event | category | flops | bytes accessed | tf_op | source)
XLA Modules:
  0.0 309.4 jit_solution(16333228598212090025)
XLA Ops:
  0.0 2.6 broadcast_in_dim.93
  2.6 9.6 %all-to-all-start = ((bf16[16,1,6,9216]{3,2,1,0:T(8,128)(2,1)}), bf16[16,1,6,9216]{3,2,1,0:T(8,128)(2,1)S(1)}, u32[]{:S(2)}, u32[]{:S(2)}) async-start(bf16[16,1,6,9216]{3,2,1,0:T(8,128)(2,1)} %broadcast_in_dim.93), calls=%async_computation | async-start | bytes 4718592 | tf_op jit(solution)/shard_map/all_to_all | solution.py:18
  12.2 55.8 %all-to-all-done = bf16[16,1,6,9216]{3,2,1,0:T(8,128)(2,1)S(1)} async-done(((bf16[16,1,6,9216]{3,2,1,0:T(8,128)(2,1)}), bf16[16,1,6,9216]{3,2,1,0:T(8,128)(2,1)S(1)}, u32[]{:S(2)}, u32[]{:S(2)}) %all-to-all-start) | async-done | bytes 1769504 | tf_op jit(solution)/shard_map/all_to_all | solution.py:18
  68.0 2.6 convert_multiply_fusion
  70.6 5.9 %reshape.293 = f32[16,6,96,96]{3,2,1,0:T(8,128)} reshape(f32[16,1,6,9216]{3,2,1,0:T(8,128)} %convert_multiply_fusion) | data formatting | bytes 7077888 | tf_op jit(solution)/shard_map/reshape | solution.py:114
  76.5 7.9 %fusion.18 = f32[16,6,96,96]{2,3,1,0:T(8,128)S(1)} fusion(f32[16,6,96,96]{3,2,1,0:T(8,128)} %reshape.293), kind=kOutput, calls=%fused_computation.33 | convolution fusion | flops 509690880 | bytes 7077888 | tf_op jit(solution)/shard_map/kz,pxyz->pxyk/dot_general | solution.py:115
  84.4 5.4 %fusion.16 = f32[16,6,96,96]{2,3,1,0:T(8,128)S(1)} fusion(f32[16,6,96,96]{3,2,1,0:T(8,128)S(1)} %copy-done), kind=kOutput, calls=%fused_computation.31 | convolution fusion | flops 509700096 | bytes 7077888 | tf_op jit(solution)/shard_map/kz,pxyz->pxyk/dot_general | solution.py:116
  89.8 2.3 fusion.23
  92.1 2.2 fusion.21
  94.3 2.9 fusion.7
  97.2 2.7 fusion.6
  100.0 3.2 %pad_maximum_fusion = bf16[2,16,6,96,96]{3,4,2,1,0:T(8,128)(2,1)} fusion(bf16[1,16,6,96,96]{3,4,2,1,0:T(8,128)(2,1)S(1)} %fusion.7, bf16[1,16,6,96,96]{3,4,2,1,0:T(8,128)(2,1)S(1)} %fusion.6), kind=kLoop, calls=%fused_computation.2 | loop fusion | flops 1769472 | bytes 7077888 | tf_op jit(solution)/shard_map/stack | solution.py:123
  103.2 9.2 %copy.84 = bf16[2,16,6,96,96]{4,1,2,0,3:T(8,128)(2,1)} copy(bf16[2,16,6,96,96]{3,4,2,1,0:T(8,128)(2,1)} %pad_maximum_fusion) | data formatting | bytes 7077888 | tf_op jit(solution)/shard_map/stack | solution.py:123
  112.4 7.3 %all-to-all-start.1 = ((bf16[2,16,6,96,96]{4,1,2,0,3:T(8,128)(2,1)}), bf16[2,16,6,96,96]{4,1,2,0,3:T(8,128)(2,1)}, u32[]{:S(2)}, u32[]{:S(2)}) async-start(bf16[2,16,6,96,96]{4,1,2,0,3:T(8,128)(2,1)} %copy.84), calls=%async_computation.1 | async-start | bytes 9437184 | tf_op jit(solution)/shard_map/all_to_all | solution.py:124
  120.4 0.2 select_reduce_fusion.2
  120.6 0.2 select_reduce_fusion
  120.9 0.2 select_reduce_fusion.1
  121.4 0.2 fusion.62
  121.6 0.2 multiply_convert_fusion
  121.9 53.6 %all-to-all-done.1 = bf16[2,16,6,96,96]{4,1,2,0,3:T(8,128)(2,1)} async-done(((bf16[2,16,6,96,96]{4,1,2,0,3:T(8,128)(2,1)}), bf16[2,16,6,96,96]{4,1,2,0,3:T(8,128)(2,1)}, u32[]{:S(2)}, u32[]{:S(2)}) %all-to-all-start.1) | async-done | bytes 3538976 | tf_op jit(solution)/shard_map/all_to_all | solution.py:124
  175.5 8.2 %copy.102 = bf16[2,16,16,6,6,96]{5,4,3,2,0,1:T(8,128)(2,1)} copy(bf16[2,16,16,6,6,96]{5,1,3,0,4,2:T(8,128)(2,1)} %bitcast.18) | data formatting | bytes 7077888 | tf_op jit(solution)/shard_map/reshape | solution.py:126
  183.8 9.6 %reshape.287 = bf16[2,16,96,576,1]{3,2,0,1,4:T(8,128)(2,1)} reshape(bf16[2,16,16,6,6,96]{5,4,3,2,0,1:T(8,128)(2,1)} %copy.102) | data formatting | bytes 7077888 | tf_op jit(solution)/shard_map/reshape | solution.py:126
  193.4 5.3 %fusion = bf16[2,16,96,576]{3,2,0,1:T(8,128)(2,1)} fusion(bf16[2,16,96,576,1]{3,2,0,1,4:T(8,128)(2,1)} %reshape.287, bf16[1,2,96,96]{3,2,1,0:T(8,128)(2,1)S(1)} %get-tuple-element.17, bf16[1,2,96,96]{3,2,1,0:T(8,128)(2,1)S(1)} %get-tuple-element.16), kind=kOutput, calls=%fused_computation.6 | convolution fusion | flops 681394176 | bytes 7151616 | tf_op jit(solution)/shard_map/orkx,rpxf->opkf/dot_general | solution.py:127
  198.7 44.3 %copy.105 = bf16[2,16,96,576]{1,0,3,2:T(2,128)(2,1)} copy(bf16[2,16,96,576]{3,2,0,1:T(8,128)(2,1)} %fusion) | data formatting | bytes 7077888 | tf_op jit(solution)/shard_map/reshape | solution.py:130
  243.0 16.1 %gather_fusion = bf16[2048,2,16]{2,1,0:T(2,128)(2,1)S(1)} fusion(bf16[2,16,55296]{1,0,2:T(2,128)(2,1)} %bitcast.91, s32[2048]{0:T(1024)S(1)} %fusion.65), kind=kCustom, calls=%fused_computation | custom fusion | bytes 270336 | tf_op jit(solution)/shard_map/jit(_take)/gather | solution.py:131
  259.1 0.7 fusion.66
  259.7 0.6 broadcast_in_dim.99
  260.4 18.7 %all-to-all-start.2 = ((bf16[16,2,16,1]{2,1,3,0:T(2,128)(2,1)}), bf16[16,2,16,1]{2,1,3,0:T(2,128)(2,1)S(1)}, u32[]{:S(2)}, u32[]{:S(2)}) async-start(bf16[16,2,16,1]{2,1,3,0:T(2,128)(2,1)} %broadcast_in_dim.99), calls=%async_computation.2 | async-start | bytes 16384 | tf_op jit(solution)/shard_map/all_to_all | solution.py:18
  279.0 7.4 %fusion.9 = bf16[2,16,2048]{1,0,2:T(2,128)(2,1)S(1)} fusion(bf16[2048,2,16]{2,1,0:T(2,128)(2,1)S(1)} %gather_fusion, pred[2048]{0:T(1024)(128)(4,1)S(1)} %compare_and_fusion), kind=kLoop, calls=%fused_computation.16 | loop fusion | flops 65536 | bytes 264192 | tf_op jit(solution)/shard_map/jit(_take)/select_n | solution.py:131
  286.9 0.4 fusion.5
  287.2 21.5 %all_to_all.30 = bf16[16,128,128]{2,1,0:T(8,128)(2,1)S(1)} all-to-all(bf16[16,128,128]{2,1,0:T(8,128)(2,1)S(1)} %bitcast.93), channel_id=1, replica_groups=mesh['band'=16,'col'=16] {'band'}, dimensions={0} | all-to-all | bytes 1048576 | tf_op jit(solution)/shard_map/all_to_all | solution.py:33
  308.7 0.7 convert_reduce_fusion
  (33 shorter events, 0.8 us)
Async XLA Ops:
  0.0 12.2 %copy-start.1 = (bf16[1,6,9216]{2,1,0:T(8,128)(2,1)S(1)}, bf16[1,6,9216]{2,1,0:T(8,128)(2,1)}, u32[]{:S(2)}) copy-start(bf16[1,6,9216]{2,1,0:T(8,128)(2,1)} %param.9) | copy-start | bytes 331780
  2.6 65.4 %all-to-all-start = ((bf16[16,1,6,9216]{3,2,1,0:T(8,128)(2,1)}), bf16[16,1,6,9216]{3,2,1,0:T(8,128)(2,1)S(1)}, u32[]{:S(2)}, u32[]{:S(2)}) async-start(bf16[16,1,6,9216]{3,2,1,0:T(8,128)(2,1)} %broadcast_in_dim.93), calls=%async_computation | async-start | bytes 4718592 | tf_op jit(solution)/shard_map/all_to_all | solution.py:18
  76.5 7.9 %copy-start = (f32[16,6,96,96]{3,2,1,0:T(8,128)S(1)}, f32[16,6,96,96]{3,2,1,0:T(8,128)}, u32[]{:S(2)}) copy-start(f32[16,6,96,96]{3,2,1,0:T(8,128)} %reshape.293) | copy-start | bytes 10616836
  112.4 8.0 %copy-start.5 = (f32[4]{0:T(128)S(1)}, f32[4]{0:T(128)}, u32[]{:S(2)}) copy-start(f32[4]{0:T(128)} %param.13) | copy-start | bytes 52
  112.4 8.1 %copy-start.6 = (f32[16]{0:T(128)S(1)}, f32[16]{0:T(128)}, u32[]{:S(2)}) copy-start(f32[16]{0:T(128)} %param.12) | copy-start | bytes 196
  112.4 8.3 %copy-start.3 = (f32[4096]{0:T(1024)S(1)}, f32[4096]{0:T(1024)}, u32[]{:S(2)}) copy-start(f32[4096]{0:T(1024)} %param.11) | copy-start | bytes 49156
  112.4 8.3 %copy-start.4 = (s32[16]{0:T(128)S(1)}, s32[16]{0:T(128)}, u32[]{:S(2)}) copy-start(s32[16]{0:T(128)} %param.10) | copy-start | bytes 196
  112.4 9.5 %copy-start.2 = (s32[2048]{0:T(1024)S(1)}, s32[2048]{0:T(1024)}, u32[]{:S(2)}) copy-start(s32[2048]{0:T(1024)} %param.14) | copy-start | bytes 24580
  112.4 63.2 %all-to-all-start.1 = ((bf16[2,16,6,96,96]{4,1,2,0,3:T(8,128)(2,1)}), bf16[2,16,6,96,96]{4,1,2,0,3:T(8,128)(2,1)}, u32[]{:S(2)}, u32[]{:S(2)}) async-start(bf16[2,16,6,96,96]{4,1,2,0,3:T(8,128)(2,1)} %copy.84), calls=%async_computation.1 | async-start | bytes 9437184 | tf_op jit(solution)/shard_map/all_to_all | solution.py:124
  260.4 26.1 %all-to-all-start.2 = ((bf16[16,2,16,1]{2,1,3,0:T(2,128)(2,1)}), bf16[16,2,16,1]{2,1,3,0:T(2,128)(2,1)S(1)}, u32[]{:S(2)}, u32[]{:S(2)}) async-start(bf16[16,2,16,1]{2,1,3,0:T(2,128)(2,1)} %broadcast_in_dim.99), calls=%async_computation.2 | async-start | bytes 16384 | tf_op jit(solution)/shard_map/all_to_all | solution.py:18
where the time goes:
time: 313 us; the launch traced here: 309 us
  waiting for transfers between devices  109 us (35%)
  local copies, waits for them, and re-layouts  97.1 us (31%)
  starting transfers between devices  35.6 us (11%)
  matrix products  29.1 us (9%)
  blocking collectives  21.5 us (7%)
  other arithmetic  15.8 us (5%)
    all_to_all x2, waiting for transfers between devices, copy_for_each(): lax.all_to_all(jnp.broadcast_to(x[None], (devices, *x.shape)), axis, 0, 0...  55.8 us
    all_to_all x1, waiting for transfers between devices, per_device(): lax.all_to_all(planes, 'col', split_axis=3, concat_axis=2, tiled=True)  53.6 us
    reshape x1, local copies, waits for them, and re-layouts, per_device(): density = density.reshape(2, items, -1)  44.3 us
    all_to_all x2, starting transfers between devices, copy_for_each(): lax.all_to_all(jnp.broadcast_to(x[None], (devices, *x.shape)), axis, 0, 0...  28.2 us
    all_to_all x1, blocking collectives, sent_and_summed(): lax.all_to_all(pieces, axis, split_axis=0, concat_axis=0, tiled=True)  21.5 us
    reshape x2, local copies, waits for them, and re-layouts, per_device(): flat = exchanged.reshape(2, items, grid_x, -1)  17.8 us
    gather x1, local copies, waits for them, and re-layouts, per_device(): row_density = jnp.take(density, gvec_cell, axis=2)  16.1 us
    another operation x1, local copies, waits for them, and re-layouts, per_device(): planes = jnp.stack([y_real, y_imag]).astype(jnp.bfloat16)  9.18 us
  transfers between devices with their start and end apart: 3, of which 2 were waited for; matrix products, arithmetic and copies ran while one was open for 3% of the time, Pallas kernels for 0%

commit v1 on v0

--- a/solution.py
+++ b/solution.py
@@ -1,3 +1,4 @@
+import functools
 import math
 import jax
 import jax.numpy as jnp
@@ -5,6 +6,21 @@
 from jax.sharding import PartitionSpec as P
 
 GY = 96
+
+
+def _remake_ports(local_array, link_axis):
+    return jnp.concatenate(
+        lax.all_to_all(
+            jnp.stack(jnp.split(local_array, lax.axis_size(link_axis), axis=3)),
+            link_axis,
+            concat_axis=0,
+            split_axis=0,
+        ),
+        axis=2,
+    )
+
+
+follow_tasks = functools.partial(_remake_ports, link_axis="col")
 
 
 def joined_along(pieces, dim):
@@ -121,7 +137,7 @@
         "jy,pxyk->pxjk", y_cosine, z_imag, precision=high
     )
     planes = jnp.stack([y_real, y_imag]).astype(jnp.bfloat16)
-    exchanged = lax.all_to_all(planes, "col", split_axis=3, concat_axis=2, tiled=True)
+    exchanged = follow_tasks(planes)
     items = exchanged.shape[1]
     flat = exchanged.reshape(2, items, grid_x, -1)
     density = jnp.einsum(

time: 313 us -> 300 us (0.958)
  local copies, waits for them, and re-layouts: 97.1 us -> 90.4 us
  matrix products: 29.1 us -> 22.6 us
    reshape x2 -> x0, local copies, waits for them, and re-layouts: 17.8 us -> none  [per_device(): flat = exchanged.reshape(2, items, grid_x, -1)]
    another operation x1 -> x3, local copies, waits for them, and re-layouts: 9.18 us -> 20.3 us  [the longest x2 16.2 us: per_device(): flat = exchanged.reshape(2, items, grid_x, -1)]
    dot_general x1, matrix products: 7.89 us -> 4.61 us  [per_device(): z_real = jnp.einsum('kz,pxyz->pxyk', z_cosine, products, precision=high)]
    dot_general x1, matrix products: 5.43 us -> 2.25 us  [per_device(): z_imag = jnp.einsum('kz,pxyz->pxyk', z_sine, products, precision=high)]
  transfers between devices with their start and end apart: 3 -> 3, of which waited for: 2 -> 2; matrix products, arithmetic and copies ran while one was open for 3% -> 8% of each run, Pallas kernels for 0% -> 0%
where the time goes in v1:
time: 300 us; the launch traced here: 296 us
  waiting for transfers between devices  109 us (36%)
  local copies, waits for them, and re-layouts  90.4 us (30%)
  starting transfers between devices  35.6 us (12%)
  matrix products  22.6 us (8%)
  blocking collectives  21.5 us (7%)
  other arithmetic  15.6 us (5%)
    all_to_all x2, waiting for transfers between devices, copy_for_each(): lax.all_to_all(jnp.broadcast_to(x[None], (devices, *x.shape)), axis, 0, 0...  55.8 us
    all_to_all x1, waiting for transfers between devices, _remake_ports(): lax.all_to_all(jnp.stack(jnp.split(local_array, lax.axis_size(link_axis),...  53.6 us
    reshape x1, local copies, waits for them, and re-layouts, per_device(): density = density.reshape(2, items, -1)  44.3 us
    all_to_all x2, starting transfers between devices, copy_for_each(): lax.all_to_all(jnp.broadcast_to(x[None], (devices, *x.shape)), axis, 0, 0...  28.3 us
    all_to_all x1, blocking collectives, sent_and_summed(): lax.all_to_all(pieces, axis, split_axis=0, concat_axis=0, tiled=True)  21.5 us
    another operation x2, local copies, waits for them, and re-layouts, per_device(): flat = exchanged.reshape(2, items, grid_x, -1)  16.2 us
    gather x1, local copies, waits for them, and re-layouts, per_device(): row_density = jnp.take(density, gvec_cell, axis=2)  16.1 us
    select_n x1, other arithmetic, per_device(): row_density = jnp.take(density, gvec_cell, axis=2)  7.45 us
  transfers between devices with their start and end apart: 3, of which 2 were waited for; matrix products, arithmetic and copies ran while one was open for 8% of the time, Pallas kernels for 0%

profile of v1, /device:TPU:2, one launch (start us, length us, event | category | flops | bytes accessed | tf_op | source)
XLA Modules:
  0.0 296.0 jit_solution(13399754177852298891)
XLA Ops:
  0.0 2.6 broadcast_in_dim.93
  2.6 9.6 %all-to-all-start = ((bf16[16,1,6,9216]{3,2,1,0:T(8,128)(2,1)}), bf16[16,1,6,9216]{3,2,1,0:T(8,128)(2,1)S(1)}, u32[]{:S(2)}, u32[]{:S(2)}) async-start(bf16[16,1,6,9216]{3,2,1,0:T(8,128)(2,1)} %broadcast_in_dim.93), calls=%async_computation | async-start | bytes 4718592 | tf_op jit(solution)/shard_map/all_to_all | solution.py:34
  12.2 55.8 %all-to-all-done = bf16[16,1,6,9216]{3,2,1,0:T(8,128)(2,1)S(1)} async-done(((bf16[16,1,6,9216]{3,2,1,0:T(8,128)(2,1)}), bf16[16,1,6,9216]{3,2,1,0:T(8,128)(2,1)S(1)}, u32[]{:S(2)}, u32[]{:S(2)}) %all-to-all-start) | async-done | bytes 1769504 | tf_op jit(solution)/shard_map/all_to_all | solution.py:34
  68.0 2.6 convert_multiply_fusion
  70.6 5.9 %reshape.292 = f32[16,6,96,96]{3,2,1,0:T(8,128)} reshape(f32[16,1,6,9216]{3,2,1,0:T(8,128)} %convert_multiply_fusion) | data formatting | bytes 7077888 | tf_op jit(solution)/shard_map/reshape | solution.py:130
  76.5 4.6 %fusion.35 = f32[16,6,96,96]{3,2,1,0:T(8,128)S(1)} fusion(f32[16,6,96,96]{3,2,1,0:T(8,128)} %reshape.292), kind=kOutput, calls=%fused_computation.95 | convolution fusion | flops 509690880 | bytes 7077888 | tf_op jit(solution)/shard_map/kz,pxyz->pxyk/dot_general | solution.py:131
  81.1 2.3 fusion.33
  83.4 2.3 fusion.38
  85.7 2.3 fusion.40
  88.0 2.7 fusion.6
  90.7 2.7 fusion.7
  93.5 0.3 bitcast_dynamic-update-slice_fusion.14
  94.5 0.2 bitcast_dynamic-update-slice_fusion.9
  95.4 0.2 bitcast_dynamic-update-slice_fusion.4
  96.5 4.1 %copy.55 = bf16[16,2,16,6,6,96]{5,2,4,3,1,0:T(8,128)(2,1)} copy(bf16[16,2,16,6,6,96]{5,4,3,2,1,0:T(8,128)(2,1)S(1)} %fusion.26) | data formatting | bytes 7077888 | tf_op jit(solution)/shard_map/stack | solution.py:14
  100.6 7.3 %all-to-all-start.1 = ((bf16[16,2,16,6,6,96]{5,2,4,3,1,0:T(8,128)(2,1)}), bf16[16,2,16,6,6,96]{5,2,4,3,1,0:T(8,128)(2,1)}, u32[]{:S(2)}, u32[]{:S(2)}) async-start(bf16[16,2,16,6,6,96]{5,2,4,3,1,0:T(8,128)(2,1)} %copy.55), calls=%async_computation.1 | async-start | bytes 9437184 | tf_op jit(solution)/shard_map/all_to_all | solution.py:13
  108.6 0.2 select_reduce_fusion
  109.6 0.2 fusion.79
  109.8 0.2 multiply_convert_fusion
  110.1 53.6 %all-to-all-done.1 = bf16[16,2,16,6,6,96]{5,2,4,3,1,0:T(8,128)(2,1)} async-done(((bf16[16,2,16,6,6,96]{5,2,4,3,1,0:T(8,128)(2,1)}), bf16[16,2,16,6,6,96]{5,2,4,3,1,0:T(8,128)(2,1)}, u32[]{:S(2)}, u32[]{:S(2)}) %all-to-all-start.1) | async-done | bytes 3538976 | tf_op jit(solution)/shard_map/all_to_all | solution.py:13
  163.7 6.6 %copy.69 = bf16[2,16,16,6,6,96]{5,4,3,2,0,1:T(8,128)(2,1)} copy(bf16[2,16,16,6,6,96]{5,1,4,3,0,2:T(8,128)(2,1)} %bitcast.32) | data formatting | bytes 7077888 | tf_op jit(solution)/shard_map/reshape;reshape | solution.py:142
  170.3 9.6 %reshape.286 = bf16[2,16,96,576,1]{3,2,0,1,4:T(8,128)(2,1)} reshape(bf16[2,16,16,6,6,96]{5,4,3,2,0,1:T(8,128)(2,1)} %copy.69) | data formatting | bytes 7077888 | tf_op jit(solution)/shard_map/reshape;reshape | solution.py:142
  180.0 5.3 %fusion = bf16[2,16,96,576]{3,2,0,1:T(8,128)(2,1)} fusion(bf16[2,16,96,576,1]{3,2,0,1,4:T(8,128)(2,1)} %reshape.286, bf16[1,2,96,96]{3,2,1,0:T(8,128)(2,1)S(1)} %get-tuple-element.17, bf16[1,2,96,96]{3,2,1,0:T(8,128)(2,1)S(1)} %get-tuple-element.16), kind=kOutput, calls=%fused_computation.35 | convolution fusion | flops 681394176 | bytes 7151616 | tf_op jit(solution)/shard_map/orkx,rpxf->opkf/dot_general | solution.py:143
  185.3 44.3 %copy.72 = bf16[2,16,96,576]{1,0,3,2:T(2,128)(2,1)} copy(bf16[2,16,96,576]{3,2,0,1:T(8,128)(2,1)} %fusion) | data formatting | bytes 7077888 | tf_op jit(solution)/shard_map/reshape | solution.py:146
  229.5 0.7 fusion.83
  230.2 0.6 broadcast_in_dim.99
  230.8 18.7 %all-to-all-start.2 = ((bf16[16,2,16,1]{2,1,3,0:T(2,128)(2,1)}), bf16[16,2,16,1]{2,1,3,0:T(2,128)(2,1)S(1)}, u32[]{:S(2)}, u32[]{:S(2)}) async-start(bf16[16,2,16,1]{2,1,3,0:T(2,128)(2,1)} %broadcast_in_dim.99), calls=%async_computation.2 | async-start | bytes 16384 | tf_op jit(solution)/shard_map/all_to_all | solution.py:34
  249.5 16.1 %gather_fusion = bf16[2048,2,16]{2,1,0:T(2,128)(2,1)S(1)} fusion(bf16[2,16,55296]{1,0,2:T(2,128)(2,1)} %bitcast.124, s32[2048]{0:T(1024)S(1)} %fusion.82), kind=kCustom, calls=%fused_computation | custom fusion | bytes 270336 | tf_op jit(solution)/shard_map/jit(_take)/gather | solution.py:147
  265.6 7.5 %fusion.9 = bf16[2,16,2048]{1,0,2:T(2,128)(2,1)S(1)} fusion(bf16[2048,2,16]{2,1,0:T(2,128)(2,1)S(1)} %gather_fusion, pred[2048]{0:T(1024)(128)(4,1)S(1)} %compare_and_fusion), kind=kLoop, calls=%fused_computation.45 | loop fusion | flops 65536 | bytes 264192 | tf_op jit(solution)/shard_map/jit(_take)/select_n | solution.py:147
  273.4 0.4 fusion.5
  273.8 21.5 %all_to_all.20 = bf16[16,128,128]{2,1,0:T(8,128)(2,1)S(1)} all-to-all(bf16[16,128,128]{2,1,0:T(8,128)(2,1)S(1)} %bitcast.125), channel_id=1, replica_groups=mesh['band'=16,'col'=16] {'band'}, dimensions={0} | all-to-all | bytes 1048576 | tf_op jit(solution)/shard_map/all_to_all | solution.py:49
  295.3 0.7 convert_reduce_fusion
  (48 shorter events, 3.4 us)
Async XLA Ops:
  0.0 12.2 %copy-start.1 = (bf16[1,6,9216]{2,1,0:T(8,128)(2,1)S(1)}, bf16[1,6,9216]{2,1,0:T(8,128)(2,1)}, u32[]{:S(2)}) copy-start(bf16[1,6,9216]{2,1,0:T(8,128)(2,1)} %param.9) | copy-start | bytes 331780
  2.6 65.4 %all-to-all-start = ((bf16[16,1,6,9216]{3,2,1,0:T(8,128)(2,1)}), bf16[16,1,6,9216]{3,2,1,0:T(8,128)(2,1)S(1)}, u32[]{:S(2)}, u32[]{:S(2)}) async-start(bf16[16,1,6,9216]{3,2,1,0:T(8,128)(2,1)} %broadcast_in_dim.93), calls=%async_computation | async-start | bytes 4718592 | tf_op jit(solution)/shard_map/all_to_all | solution.py:34
  76.5 4.6 %copy-start = (f32[16,6,96,96]{3,2,1,0:T(8,128)S(1)}, f32[16,6,96,96]{3,2,1,0:T(8,128)}, u32[]{:S(2)}) copy-start(f32[16,6,96,96]{3,2,1,0:T(8,128)} %reshape.292) | copy-start | bytes 10616836
  100.5 8.0 %copy-start.5 = (f32[4]{0:T(128)S(1)}, f32[4]{0:T(128)}, u32[]{:S(2)}) copy-start(f32[4]{0:T(128)} %param.13) | copy-start | bytes 52
  100.5 8.1 %copy-start.3 = (f32[4096]{0:T(1024)S(1)}, f32[4096]{0:T(1024)}, u32[]{:S(2)}) copy-start(f32[4096]{0:T(1024)} %param.11) | copy-start | bytes 49156
  100.5 8.1 %copy-start.4 = (s32[16]{0:T(128)S(1)}, s32[16]{0:T(128)}, u32[]{:S(2)}) copy-start(s32[16]{0:T(128)} %param.10) | copy-start | bytes 196
  100.5 8.5 %copy-start.6 = (f32[16]{0:T(128)S(1)}, f32[16]{0:T(128)}, u32[]{:S(2)}) copy-start(f32[16]{0:T(128)} %param.12) | copy-start | bytes 196
  100.6 9.5 %copy-start.2 = (s32[2048]{0:T(1024)S(1)}, s32[2048]{0:T(1024)}, u32[]{:S(2)}) copy-start(s32[2048]{0:T(1024)} %param.14) | copy-start | bytes 24580
  100.6 63.2 %all-to-all-start.1 = ((bf16[16,2,16,6,6,96]{5,2,4,3,1,0:T(8,128)(2,1)}), bf16[16,2,16,6,6,96]{5,2,4,3,1,0:T(8,128)(2,1)}, u32[]{:S(2)}, u32[]{:S(2)}) async-start(bf16[16,2,16,6,6,96]{5,2,4,3,1,0:T(8,128)(2,1)} %copy.55), calls=%async_computation.1 | async-start | bytes 9437184 | tf_op jit(solution)/shard_map/all_to_all | solution.py:13
  230.8 42.3 %all-to-all-start.2 = ((bf16[16,2,16,1]{2,1,3,0:T(2,128)(2,1)}), bf16[16,2,16,1]{2,1,3,0:T(2,128)(2,1)S(1)}, u32[]{:S(2)}, u32[]{:S(2)}) async-start(bf16[16,2,16,1]{2,1,3,0:T(2,128)(2,1)} %broadcast_in_dim.99), calls=%async_computation.2 | async-start | bytes 16384 | tf_op jit(solution)/shard_map/all_to_all | solution.py:34
